TPU v7x, 512 devices: a whole 4x8x8 slice. The times are simulated.
512 devices in a mesh: angle: 8 (over x, core), gx: 16 (over y, z_lo), gy: 4 (over z_hi).
Axes of the slice: x: 4, y: 8, z: 8 (z_hi: 4, z_lo: 2; z = z_hi * 2 + z_lo), core: 2. Of those that a mesh axis runs over, the one named last changes fastest.
Arguments:
- forward_fields: float32 [8, 12, 128, 64, 128], P('angle', None, 'gx', 'gy'), may hold values from -6 to 6
- adjoint_fields: float32 [8, 12, 128, 64, 128], P('angle', None, 'gx', 'gy'), may hold values from -6 to 6
- forward_spectrum: float32 [8, 6, 128, 64, 128], P('angle', None, 'gx', 'gy'), may hold values from -6 to 6
- adjoint_spectrum: float32 [8, 6, 128, 64, 128], P('angle', None, 'gx', 'gy'), may hold values from -6 to 6
- permittivity: float32 [128, 64, 128], P('gx', 'gy'), may hold values from 1 to 12
- phase_table: float32 [8, 2], replicated, may hold values from -3.140625 to 3.140625
- angle_index: int32 [8], P('angle'), may hold values from 0 to 7, each once
- design_tiles: int32 [16], replicated, may hold values from 0 to 63, as said below
Outputs:
- forward_transform: float32 [8, 6, 128, 64, 128], P('angle', None, 'gx', 'gy')
- adjoint_transform: float32 [8, 6, 128, 64, 128], P('angle', None, 'gx', 'gy')
- gradient: float32 [128, 64, 128], P('gx', 'gy', 'angle')
Inputs may be any that keep to these rules, and one draw needn't show every extreme that they name: `angle_index`: every row of phase_table is used by exactly one angle. `design_tiles`: 16 distinct tile numbers; tiles 0 and 63 are always among them.
All inputs are finite; a program needn't handle non-finite values.
Results may differ from a plain program's by a relative error of at most 0.0001.
Values sent between devices are 32-bit elements; how exact they have to be, the bound alone decides.
A program may use at most 64 MiB of HBM per device.

v0:
```python
import math
import jax
import jax.numpy as jnp
from jax import lax
from jax.sharding import PartitionSpec as P

STEPS = 3
courant = 0.5
omega_step = 0.7


def from_behind(value, axis, steps):
    count = lax.axis_size(axis)
    pairs = [(source, (source + steps) % count) for source in range(count)]
    return lax.ppermute(value, axis, pairs)


def rotate_runs(pair, cosine, sine):
    sine_full = sine.reshape((2,) + (1,) * (pair.ndim - 2))
    real_part = pair[:, 0]
    imag_part = pair[:, 1]
    return jnp.stack(
        [real_part * cosine - imag_part * sine_full, real_part * sine_full + imag_part * cosine],
        axis=1,
    )


def next_depth(field):
    return jnp.concatenate([field[..., 1:], jnp.zeros_like(field[..., :1])], axis=-1)


def prev_depth(field):
    return jnp.concatenate([jnp.zeros_like(field[..., :1]), field[..., :-1]], axis=-1)


def curl_forward(efield, phases):
    cos_x, sine_x, cos_y, sine_y = phases
    place_x = lax.axis_index("gx")
    place_y = lax.axis_index("gy")
    last_x = lax.axis_size("gx") - 1
    last_y = lax.axis_size("gy") - 1
    send_x = efield[:, :, 1:3, 0]
    got_x = from_behind(send_x, "gx", -1)
    got_x = jnp.where(place_x == last_x, rotate_runs(got_x, cos_x, sine_x), got_x)
    send_y = jnp.stack([efield[:, :, 0, :, 0], efield[:, :, 2, :, 0]], axis=2)
    got_y = from_behind(send_y, "gy", -1)
    got_y = jnp.where(place_y == last_y, rotate_runs(got_y, cos_y, sine_y), got_y)
    comp_x = efield[:, :, 0]
    comp_y = efield[:, :, 1]
    comp_z = efield[:, :, 2]
    dz_dy = jnp.concatenate([comp_z[:, :, :, 1:], got_y[:, :, 1][:, :, :, None]], axis=3) - comp_z
    dy_dz = next_depth(comp_y) - comp_y
    dx_dz = next_depth(comp_x) - comp_x
    dz_dx = jnp.concatenate([comp_z[:, :, 1:], got_x[:, :, 1][:, :, None]], axis=2) - comp_z
    dy_dx = jnp.concatenate([comp_y[:, :, 1:], got_x[:, :, 0][:, :, None]], axis=2) - comp_y
    dx_dy = jnp.concatenate([comp_x[:, :, :, 1:], got_y[:, :, 0][:, :, :, None]], axis=3) - comp_x
    return jnp.stack([dz_dy - dy_dz, dx_dz - dz_dx, dy_dx - dx_dy], axis=2)


def curl_backward(hfield, phases):
    cos_x, sine_x, cos_y, sine_y = phases
    place_x = lax.axis_index("gx")
    place_y = lax.axis_index("gy")
    send_x = hfield[:, :, 1:3, -1]
    got_x = from_behind(send_x, "gx", 1)
    got_x = jnp.where(place_x == 0, rotate_runs(got_x, cos_x, -sine_x), got_x)
    send_y = jnp.stack([hfield[:, :, 0, :, -1], hfield[:, :, 2, :, -1]], axis=2)
    got_y = from_behind(send_y, "gy", 1)
    got_y = jnp.where(place_y == 0, rotate_runs(got_y, cos_y, -sine_y), got_y)
    comp_x = hfield[:, :, 0]
    comp_y = hfield[:, :, 1]
    comp_z = hfield[:, :, 2]
    hz_below_y = jnp.concatenate([got_y[:, :, 1][:, :, :, None], comp_z[:, :, :, :-1]], axis=3)
    hx_below_y = jnp.concatenate([got_y[:, :, 0][:, :, :, None], comp_x[:, :, :, :-1]], axis=3)
    hz_below_x = jnp.concatenate([got_x[:, :, 1][:, :, None], comp_z[:, :, :-1]], axis=2)
    hy_below_x = jnp.concatenate([got_x[:, :, 0][:, :, None], comp_y[:, :, :-1]], axis=2)
    first = comp_z - hz_below_y - (comp_y - prev_depth(comp_y))
    second = comp_x - prev_depth(comp_x) - (comp_z - hz_below_x)
    third = comp_y - hy_below_x - (comp_x - hx_below_y)
    return jnp.stack([first, second, third], axis=2)


def shards(
    forward_fields,
    adjoint_fields,
    forward_spectrum,
    adjoint_spectrum,
    permittivity,
    phase_table,
    angle_index,
    design_tiles,
):
    cells = forward_fields.shape[2:]
    fields = jnp.concatenate([forward_fields, adjoint_fields], axis=0)
    spectrum = jnp.concatenate([forward_spectrum, adjoint_spectrum], axis=0).reshape(
        (2, 2, 3) + cells
    )
    table_rows = phase_table.shape[0]
    picked = (jnp.arange(table_rows) == angle_index[0]).astype(jnp.float32)
    angle_x = jnp.sum(picked * phase_table[:, 0])
    angle_y = jnp.sum(picked * phase_table[:, 1])
    run_sign = jnp.array([1.0, -1.0], jnp.float32)
    efield = fields[:, 0:6].reshape((2, 2, 3) + cells)
    hfield = fields[:, 6:12].reshape((2, 2, 3) + cells)
    phases = (
        jnp.cos(angle_x),
        run_sign * jnp.sin(angle_x),
        jnp.cos(angle_y),
        run_sign * jnp.sin(angle_y),
    )
    coef = courant / permittivity
    for step in range(STEPS):
        hfield = hfield - courant * curl_forward(efield, phases)
        efield = efield + coef * curl_backward(hfield, phases)
        theta = omega_step * (step + 1)
        spectrum = spectrum + rotate_runs(
            efield, math.cos(theta), jnp.full((2,), math.sin(theta), jnp.float32)
        )
    local_term = jnp.sum(spectrum[0, 0] * spectrum[1, 0] - spectrum[0, 1] * spectrum[1, 1], axis=0)
    own_tile = lax.axis_index("gx") * lax.axis_size("gy") + lax.axis_index("gy")
    chosen = jnp.any(design_tiles == own_tile)
    local_term = jnp.where(chosen, local_term, jnp.zeros_like(local_term))
    groups = lax.axis_size("angle")
    whole = lax.psum(local_term, "angle")
    share = whole.shape[2] // groups
    summed = lax.dynamic_slice_in_dim(whole, lax.axis_index("angle") * share, share, 2)
    gradient = summed * (1.0 / groups)
    forward_out = spectrum[0].reshape((1, 6) + cells)
    adjoint_out = spectrum[1].reshape((1, 6) + cells)
    return (forward_out, adjoint_out, gradient)


def solution(mesh):
    in_specs = (
        P("angle", None, "gx", "gy", None),
        P("angle", None, "gx", "gy", None),
        P("angle", None, "gx", "gy", None),
        P("angle", None, "gx", "gy", None),
        P("gx", "gy", None),
        P(),
        P("angle"),
        P(),
    )
    out_specs = (
        P("angle", None, "gx", "gy", None),
        P("angle", None, "gx", "gy", None),
        P("gx", "gy", "angle"),
    )
    return jax.shard_map(shards, mesh=mesh, in_specs=in_specs, out_specs=out_specs, check_vma=False)
```

profile of v0, /device:TPU:8, one launch (start us, length us, event | category | flops | bytes accessed | tf_op | source)
XLA Modules:
  0.0 201.6 jit_solution(371373391882974185)
XLA Ops:
  7.2 1.3 constant_dynamic-update-slice_fusion.1
  9.4 11.1 %collective-permute-start = (f32[2,2,2,8,128]{4,1,0,3,2:T(2,128)}, f32[2,2,2,8,128]{4,1,0,3,2:T(2,128)}, u32[]{:S(2)}, u32[]{:S(2)}) collective-permute-start(f32[2,2,2,8,128]{4,1,0,3,2:T(2,128)} %pad_maximum_fusion.1), channel_id=1, source_target_pairs={{0,3},{1,0},{2,1},{3,2},{4,7},{5,4},{6,5},{7,6},{8,11},{9,8},{10,9... | collective-permute-start | bytes 98312 | tf_op jit(solution)/shard_map/ppermute | solution.py:15
  21.8 3.3 %collective-permute-start.1 = (f32[2,2,2,16,128]{4,1,0,3,2:T(2,128)}, f32[2,2,2,16,128]{4,1,0,3,2:T(2,128)S(1)}, u32[]{:S(2)}, u32[]{:S(2)}) collective-permute-start(f32[2,2,2,16,128]{4,1,0,3,2:T(2,128)} %slice_bitcast_fusion.25), channel_id=1, source_target_pairs={{0,60},{4,0},{8,4},{12,8},{16,12},{20,16},{24,20},{28,24},{32,28},... | collective-permute-start | bytes 196616 | tf_op jit(solution)/shard_map/ppermute | solution.py:15
  27.8 1.1 copy_bitcast_fusion.2
  28.9 0.8 slice_bitcast_fusion.14
  30.3 0.9 broadcast_divide_fusion
  31.2 1.2 pad_maximum_fusion
  33.1 1.4 compare_reduce_fusion
  35.7 2.0 %slice.554 = f32[2,2,8,16,127]{4,1,0,3,2:T(2,128)} slice(f32[2,2,8,16,128]{4,1,0,3,2:T(2,128)} %copy-done.4), slice={[0:2], [0:2], [0:8], [0:16], [1:128]} | slice | bytes 520192 | tf_op jit(solution)/shard_map/slice | solution.py:29
  37.8 1.7 slice.547
  39.4 1.6 slice.557
  41.1 1.0 slice.556
  42.1 1.0 multiply_subtract_fusion.14
  43.1 0.8 maximum_select_fusion.6
  44.2 1.4 fusion.11
  45.7 0.7 fusion.7
  46.4 0.9 fusion
  47.5 2.6 %collective-permute-start.3 = (f32[2,2,2,16,128]{4,1,0,3,2:T(2,128)S(1)}, f32[2,2,2,16,128]{4,1,0,3,2:T(2,128)S(1)}, u32[]{:S(2)}, u32[]{:S(2)}) collective-permute-start(f32[2,2,2,16,128]{4,1,0,3,2:T(2,128)S(1)} %slice_bitcast_fusion.24), channel_id=1, source_target_pairs={{0,4},{4,8},{8,12},{12,16},{16,20},{20,24},{24,28},{28,32},{32,36}... | collective-permute-start | bytes 196616 | tf_op jit(solution)/shard_map/ppermute | solution.py:15
  50.1 1.9 collective-permute-start.2
  52.1 5.9 %collective-permute-done.2 = f32[2,2,2,8,128]{4,1,0,3,2:T(2,128)S(1)} collective-permute-done((f32[2,2,2,8,128]{4,1,0,3,2:T(2,128)S(1)}, f32[2,2,2,8,128]{4,1,0,3,2:T(2,128)S(1)}, u32[]{:S(2)}, u32[]{:S(2)}) %collective-permute-start.2) | collective-permute-done | bytes 32800 | tf_op jit(solution)/shard_map/ppermute | solution.py:15
  58.9 0.8 fusion.14
  59.7 0.8 fusion.1
  60.8 1.1 multiply_subtract_fusion.2
  61.9 1.9 collective-permute-start.4
  64.6 4.5 %collective-permute-start.5 = (f32[2,2,2,16,128]{4,1,0,3,2:T(2,128)S(1)}, f32[2,2,2,16,128]{4,1,0,3,2:T(2,128)S(1)}, u32[]{:S(2)}, u32[]{:S(2)}) collective-permute-start(f32[2,2,2,16,128]{4,1,0,3,2:T(2,128)S(1)} %slice_bitcast_fusion.23), channel_id=1, source_target_pairs={{0,60},{4,0},{8,4},{12,8},{16,12},{20,16},{24,20},{28,24},{32,28},... | collective-permute-start | bytes 196616 | tf_op jit(solution)/shard_map/ppermute | solution.py:15
  69.2 1.9 collective-permute-done.5
  72.9 0.9 copy_subtract_fusion.1
  74.2 4.8 %collective-permute-start.6 = (f32[2,2,2,8,128]{4,3,2,1,0:T(8,128)S(1)}, f32[2,2,2,8,128]{4,3,2,1,0:T(8,128)S(1)}, u32[]{:S(2)}, u32[]{:S(2)}) collective-permute-start(f32[2,2,2,8,128]{4,3,2,1,0:T(8,128)S(1)} %pad_maximum_fusion.4), channel_id=1, source_target_pairs={{0,1},{1,2},{2,3},{3,0},{4,5},{5,6},{6,7},{7,4},{8,9},{9,10},{10,1... | collective-permute-start | bytes 98312 | tf_op jit(solution)/shard_map/ppermute | solution.py:15
  79.0 4.8 %collective-permute-start.7 = (f32[2,2,2,16,128]{4,1,0,3,2:T(2,128)S(1)}, f32[2,2,2,16,128]{4,1,0,3,2:T(2,128)S(1)}, u32[]{:S(2)}, u32[]{:S(2)}) collective-permute-start(f32[2,2,2,16,128]{4,1,0,3,2:T(2,128)S(1)} %bitcast.365), channel_id=1, source_target_pairs={{0,4},{4,8},{8,12},{12,16},{16,20},{20,24},{24,28},{28,32},{32,36}... | collective-permute-start | bytes 196616 | tf_op jit(solution)/shard_map/ppermute | solution.py:15
  84.3 1.7 collective-permute-done.7
  86.6 0.8 fusion.28
  87.4 1.1 fusion.4
  88.7 1.1 multiply_subtract_fusion.1
  89.9 3.1 %collective-permute-start.8 = (f32[2,2,2,8,128]{4,1,0,3,2:T(2,128)S(1)}, f32[2,2,2,8,128]{4,1,0,3,2:T(2,128)S(1)}, u32[]{:S(2)}, u32[]{:S(2)}) collective-permute-start(f32[2,2,2,8,128]{4,1,0,3,2:T(2,128)S(1)} %pad_maximum_fusion.5), channel_id=1, source_target_pairs={{0,3},{1,0},{2,1},{3,2},{4,7},{5,4},{6,5},{7,6},{8,11},{9,8},{10,9... | collective-permute-start | bytes 98312 | tf_op jit(solution)/shard_map/ppermute | solution.py:15
  93.7 4.7 %collective-permute-start.9 = (f32[2,2,2,16,128]{4,1,0,3,2:T(2,128)S(1)}, f32[2,2,2,16,128]{4,1,0,3,2:T(2,128)S(1)}, u32[]{:S(2)}, u32[]{:S(2)}) collective-permute-start(f32[2,2,2,16,128]{4,1,0,3,2:T(2,128)S(1)} %slice_bitcast_fusion.22), channel_id=1, source_target_pairs={{0,60},{4,0},{8,4},{12,8},{16,12},{20,16},{24,20},{28,24},{32,28},... | collective-permute-start | bytes 196616 | tf_op jit(solution)/shard_map/ppermute | solution.py:15
  98.6 1.7 collective-permute-done.9
  102.9 3.6 %collective-permute-start.10 = (f32[2,2,2,8,128]{4,3,2,1,0:T(8,128)S(1)}, f32[2,2,2,8,128]{4,3,2,1,0:T(8,128)S(1)}, u32[]{:S(2)}, u32[]{:S(2)}) collective-permute-start(f32[2,2,2,8,128]{4,3,2,1,0:T(8,128)S(1)} %copy.222), channel_id=1, source_target_pairs={{0,1},{1,2},{2,3},{3,0},{4,5},{5,6},{6,7},{7,4},{8,9},{9,10},{10,1... | collective-permute-start | bytes 98312 | tf_op jit(solution)/shard_map/ppermute | solution.py:15
  106.5 4.6 %collective-permute-start.11 = (f32[2,2,2,16,128]{4,1,0,3,2:T(2,128)S(1)}, f32[2,2,2,16,128]{4,1,0,3,2:T(2,128)S(1)}, u32[]{:S(2)}, u32[]{:S(2)}) collective-permute-start(f32[2,2,2,16,128]{4,1,0,3,2:T(2,128)S(1)} %bitcast.364), channel_id=1, source_target_pairs={{0,4},{4,8},{8,12},{12,16},{16,20},{20,24},{24,28},{28,32},{32,36}... | collective-permute-start | bytes 196616 | tf_op jit(solution)/shard_map/ppermute | solution.py:15
  111.6 3.5 %collective-permute-done.11 = f32[2,2,2,16,128]{4,1,0,3,2:T(2,128)S(1)} collective-permute-done((f32[2,2,2,16,128]{4,1,0,3,2:T(2,128)S(1)}, f32[2,2,2,16,128]{4,1,0,3,2:T(2,128)S(1)}, u32[]{:S(2)}, u32[]{:S(2)}) %collective-permute-start.11) | collective-permute-done | bytes 65568 | tf_op jit(solution)/shard_map/ppermute | solution.py:15
  115.7 0.8 fusion.41
  116.5 1.3 fusion.5
  117.8 1.1 multiply_subtract_fusion
  118.9 2.4 %fusion.3 = f32[2,2,3,8,16,128]{5,1,0,4,2,3:T(2,128)S(1)} fusion(f32[2,1,3,8,16,128]{5,1,0,4,2,3:T(1,128)S(1)} %get-tuple-element.40, f32[2,1,3,8,16,128]{5,1,0,4,2,3:T(1,128)S(1)} %get-tuple-element.39, f32[2,1,3,8,16,128]{5,1,0,4,2,3:T(1,128)S(1)} %get-tuple-element.25, f32[2,1,3,8,16,128]{5,1,0,4,2,3:T(1,128)S(1)} %get-tuple-element.24, ...), kind=kLoop, calls=%fused_computation.7 | loop fusion | flops 1179648 | bytes 3932160 | tf_op jit(solution)/shard_map/add | solution.py:116
  121.8 1.3 broadcast_select_fusion
  123.5 0.8 copy.232
  124.3 0.8 copy.233
  125.1 68.1 %all-reduce.14.cloned.1.call-done = f32[8,16,128]{2,1,0:T(8,128)} async-done(((f32[8,16,128]{2,1,0:T(8,128)}), f32[8,16,128]{2,1,0:T(8,128)}) %all-reduce.14.cloned.1.call-update) | async-done | bytes 65552 | tf_op jit(solution)/shard_map/psum | solution.py:124
  193.2 1.6 dynamic-slice_multiply_fusion
  (144 shorter events, 15.3 us)
Async XLA Ops:
  7.2 1.4 copy-start.9
  7.2 186.1 %all-reduce.14.cloned.1.call-start = ((), (), s32[]{:S(2)}) async-start(), calls=%async_computation | async-start | bytes 131072 | tf_op jit(solution)/shard_map/psum | solution.py:124
  9.4 16.4 %copy-start.10 = (f32[8,2]{0,1:T(2,128)S(1)}, f32[8,2]{0,1:T(2,128)}, u32[]{:S(2)}) copy-start(f32[8,2]{0,1:T(2,128)} %param.14) | copy-start | bytes 196
  9.4 32.7 %collective-permute-start = (f32[2,2,2,8,128]{4,1,0,3,2:T(2,128)}, f32[2,2,2,8,128]{4,1,0,3,2:T(2,128)}, u32[]{:S(2)}, u32[]{:S(2)}) collective-permute-start(f32[2,2,2,8,128]{4,1,0,3,2:T(2,128)} %pad_maximum_fusion.1), channel_id=1, source_target_pairs={{0,3},{1,0},{2,1},{3,2},{4,7},{5,4},{6,5},{7,6},{8,11},{9,8},{10,9... | collective-permute-start | bytes 98312 | tf_op jit(solution)/shard_map/ppermute | solution.py:15
  21.8 22.2 %collective-permute-start.1 = (f32[2,2,2,16,128]{4,1,0,3,2:T(2,128)}, f32[2,2,2,16,128]{4,1,0,3,2:T(2,128)S(1)}, u32[]{:S(2)}, u32[]{:S(2)}) collective-permute-start(f32[2,2,2,16,128]{4,1,0,3,2:T(2,128)} %slice_bitcast_fusion.25), channel_id=1, source_target_pairs={{0,60},{4,0},{8,4},{12,8},{16,12},{20,16},{24,20},{28,24},{32,28},... | collective-permute-start | bytes 196616 | tf_op jit(solution)/shard_map/ppermute | solution.py:15
  25.1 5.3 %copy-start = (f32[2,2,1,8,16,128]{5,4,3,2,1,0:T(8,128)}, f32[2,2,1,8,16,128]{5,4,3,2,1,0:T(8,128)S(1)}, u32[]{:S(2)}) copy-start(f32[2,2,1,8,16,128]{5,4,3,2,1,0:T(8,128)S(1)} %get-tuple-element.49) | copy-start | bytes 786436
  25.1 5.2 %copy-start.2 = (f32[2,2,8,16,128]{4,1,0,3,2:T(2,128)}, f32[2,2,8,16,128]{4,1,0,3,2:T(2,128)S(1)}, u32[]{:S(2)}) copy-start(f32[2,2,8,16,128]{4,1,0,3,2:T(2,128)S(1)} %slice_bitcast_fusion.21) | copy-start | bytes 786436
  28.9 1.5 copy-start.4
  35.7 5.3 %copy-start.3 = (f32[2,2,8,16,128]{4,1,0,3,2:T(2,128)S(1)}, f32[2,2,8,16,128]{4,1,0,3,2:T(2,128)}, u32[]{:S(2)}) copy-start(f32[2,2,8,16,128]{4,1,0,3,2:T(2,128)} %copy-done.2) | copy-start | bytes 786436
  42.1 3.5 %copy-start.1 = (f32[2,2,1,8,16,128]{5,4,3,2,1,0:T(8,128)S(1)}, f32[2,2,1,8,16,128]{5,4,3,2,1,0:T(8,128)}, u32[]{:S(2)}) copy-start(f32[2,2,1,8,16,128]{5,4,3,2,1,0:T(8,128)} %copy-done) | copy-start | bytes 786436
  42.1 3.5 %copy-start.5 = (f32[2,2,8,16,127]{4,1,0,3,2:T(2,128)S(1)}, f32[2,2,8,16,127]{4,1,0,3,2:T(2,128)}, u32[]{:S(2)}) copy-start(f32[2,2,8,16,127]{4,1,0,3,2:T(2,128)} %slice.554) | copy-start | bytes 780292
  42.1 3.5 %copy-start.6 = (f32[2,2,8,16,127]{4,1,0,3,2:T(2,128)S(1)}, f32[2,2,8,16,127]{4,1,0,3,2:T(2,128)}, u32[]{:S(2)}) copy-start(f32[2,2,8,16,127]{4,1,0,3,2:T(2,128)} %slice.556) | copy-start | bytes 780292
  42.1 3.5 %copy-start.7 = (f32[2,2,8,15,128]{4,1,0,3,2:T(2,128)S(1)}, f32[2,2,8,15,128]{4,1,0,3,2:T(2,128)}, u32[]{:S(2)}) copy-start(f32[2,2,8,15,128]{4,1,0,3,2:T(2,128)} %slice.547) | copy-start | bytes 737284
  42.1 3.5 %copy-start.8 = (f32[2,2,7,16,128]{4,1,0,3,2:T(2,128)S(1)}, f32[2,2,7,16,128]{4,1,0,3,2:T(2,128)}, u32[]{:S(2)}) copy-start(f32[2,2,7,16,128]{4,1,0,3,2:T(2,128)} %slice.557) | copy-start | bytes 688132
  47.5 10.7 %collective-permute-start.3 = (f32[2,2,2,16,128]{4,1,0,3,2:T(2,128)S(1)}, f32[2,2,2,16,128]{4,1,0,3,2:T(2,128)S(1)}, u32[]{:S(2)}, u32[]{:S(2)}) collective-permute-start(f32[2,2,2,16,128]{4,1,0,3,2:T(2,128)S(1)} %slice_bitcast_fusion.24), channel_id=1, source_target_pairs={{0,4},{4,8},{8,12},{12,16},{16,20},{20,24},{24,28},{28,32},{32,36}... | collective-permute-start | bytes 196616 | tf_op jit(solution)/shard_map/ppermute | solution.py:15
  50.1 7.9 %collective-permute-start.2 = (f32[2,2,2,8,128]{4,1,0,3,2:T(2,128)S(1)}, f32[2,2,2,8,128]{4,1,0,3,2:T(2,128)S(1)}, u32[]{:S(2)}, u32[]{:S(2)}) collective-permute-start(f32[2,2,2,8,128]{4,1,0,3,2:T(2,128)S(1)} %pad_maximum_fusion.2), channel_id=1, source_target_pairs={{0,1},{1,2},{2,3},{3,0},{4,5},{5,6},{6,7},{7,4},{8,9},{9,10},{10,1... | collective-permute-start | bytes 98312 | tf_op jit(solution)/shard_map/ppermute | solution.py:15
  61.9 7.1 %collective-permute-start.4 = (f32[2,2,2,8,128]{4,1,0,3,2:T(2,128)S(1)}, f32[2,2,2,8,128]{4,1,0,3,2:T(2,128)S(1)}, u32[]{:S(2)}, u32[]{:S(2)}) collective-permute-start(f32[2,2,2,8,128]{4,1,0,3,2:T(2,128)S(1)} %pad_maximum_fusion.3), channel_id=1, source_target_pairs={{0,3},{1,0},{2,1},{3,2},{4,7},{5,4},{6,5},{7,6},{8,11},{9,8},{10,9... | collective-permute-start | bytes 98312 | tf_op jit(solution)/shard_map/ppermute | solution.py:15
  64.6 6.5 %collective-permute-start.5 = (f32[2,2,2,16,128]{4,1,0,3,2:T(2,128)S(1)}, f32[2,2,2,16,128]{4,1,0,3,2:T(2,128)S(1)}, u32[]{:S(2)}, u32[]{:S(2)}) collective-permute-start(f32[2,2,2,16,128]{4,1,0,3,2:T(2,128)S(1)} %slice_bitcast_fusion.23), channel_id=1, source_target_pairs={{0,60},{4,0},{8,4},{12,8},{16,12},{20,16},{24,20},{28,24},{32,28},... | collective-permute-start | bytes 196616 | tf_op jit(solution)/shard_map/ppermute | solution.py:15
  74.2 10.0 %collective-permute-start.6 = (f32[2,2,2,8,128]{4,3,2,1,0:T(8,128)S(1)}, f32[2,2,2,8,128]{4,3,2,1,0:T(8,128)S(1)}, u32[]{:S(2)}, u32[]{:S(2)}) collective-permute-start(f32[2,2,2,8,128]{4,3,2,1,0:T(8,128)S(1)} %pad_maximum_fusion.4), channel_id=1, source_target_pairs={{0,1},{1,2},{2,3},{3,0},{4,5},{5,6},{6,7},{7,4},{8,9},{9,10},{10,1... | collective-permute-start | bytes 98312 | tf_op jit(solution)/shard_map/ppermute | solution.py:15
  79.0 7.1 %collective-permute-start.7 = (f32[2,2,2,16,128]{4,1,0,3,2:T(2,128)S(1)}, f32[2,2,2,16,128]{4,1,0,3,2:T(2,128)S(1)}, u32[]{:S(2)}, u32[]{:S(2)}) collective-permute-start(f32[2,2,2,16,128]{4,1,0,3,2:T(2,128)S(1)} %bitcast.365), channel_id=1, source_target_pairs={{0,4},{4,8},{8,12},{12,16},{16,20},{20,24},{24,28},{28,32},{32,36}... | collective-permute-start | bytes 196616 | tf_op jit(solution)/shard_map/ppermute | solution.py:15
  89.9 8.6 %collective-permute-start.8 = (f32[2,2,2,8,128]{4,1,0,3,2:T(2,128)S(1)}, f32[2,2,2,8,128]{4,1,0,3,2:T(2,128)S(1)}, u32[]{:S(2)}, u32[]{:S(2)}) collective-permute-start(f32[2,2,2,8,128]{4,1,0,3,2:T(2,128)S(1)} %pad_maximum_fusion.5), channel_id=1, source_target_pairs={{0,3},{1,0},{2,1},{3,2},{4,7},{5,4},{6,5},{7,6},{8,11},{9,8},{10,9... | collective-permute-start | bytes 98312 | tf_op jit(solution)/shard_map/ppermute | solution.py:15
  93.7 6.6 %collective-permute-start.9 = (f32[2,2,2,16,128]{4,1,0,3,2:T(2,128)S(1)}, f32[2,2,2,16,128]{4,1,0,3,2:T(2,128)S(1)}, u32[]{:S(2)}, u32[]{:S(2)}) collective-permute-start(f32[2,2,2,16,128]{4,1,0,3,2:T(2,128)S(1)} %slice_bitcast_fusion.22), channel_id=1, source_target_pairs={{0,60},{4,0},{8,4},{12,8},{16,12},{20,16},{24,20},{28,24},{32,28},... | collective-permute-start | bytes 196616 | tf_op jit(solution)/shard_map/ppermute | solution.py:15
  102.9 8.6 %collective-permute-start.10 = (f32[2,2,2,8,128]{4,3,2,1,0:T(8,128)S(1)}, f32[2,2,2,8,128]{4,3,2,1,0:T(8,128)S(1)}, u32[]{:S(2)}, u32[]{:S(2)}) collective-permute-start(f32[2,2,2,8,128]{4,3,2,1,0:T(8,128)S(1)} %copy.222), channel_id=1, source_target_pairs={{0,1},{1,2},{2,3},{3,0},{4,5},{5,6},{6,7},{7,4},{8,9},{9,10},{10,1... | collective-permute-start | bytes 98312 | tf_op jit(solution)/shard_map/ppermute | solution.py:15
  106.5 8.6 %collective-permute-start.11 = (f32[2,2,2,16,128]{4,1,0,3,2:T(2,128)S(1)}, f32[2,2,2,16,128]{4,1,0,3,2:T(2,128)S(1)}, u32[]{:S(2)}, u32[]{:S(2)}) collective-permute-start(f32[2,2,2,16,128]{4,1,0,3,2:T(2,128)S(1)} %bitcast.364), channel_id=1, source_target_pairs={{0,4},{4,8},{8,12},{12,16},{16,20},{20,24},{24,28},{28,32},{32,36}... | collective-permute-start | bytes 196616 | tf_op jit(solution)/shard_map/ppermute | solution.py:15
Sparse Core Ops, SparseCore 0:
  123.2 69.9 all-reduce.13
where the time goes:
time: 202 us
  waiting for transfers between devices  82.9 us (41%)
  starting transfers between devices  50.9 us (25%)
  other arithmetic  31.9 us (16%)
  between operations  18.5 us (9%)
  local copies, waits for them, and re-layouts  17.4 us (9%)
    psum x1, waiting for transfers between devices, shards(): whole = lax.psum(local_term, 'angle')  68.1 us
    ppermute x12, starting transfers between devices, from_behind(): return lax.ppermute(value, axis, pairs)  50.9 us
    ppermute x12, waiting for transfers between devices, from_behind(): return lax.ppermute(value, axis, pairs)  14.8 us
    sub x15, other arithmetic, rotate_runs(): real_part * cosine - imag_part * sine_full  5.45 us
    slice x6, local copies, waits for them, and re-layouts, next_depth(): field[..., 1:]  4.42 us
  transfers between devices with their start and end apart: 13, of which 6 were waited for; matrix products, arithmetic and copies ran while one was open for 11% of the time, Pallas kernels for 0%

commit v1 on v0

--- a/solution.py
+++ b/solution.py
@@ -121,7 +121,9 @@
     chosen = jnp.any(design_tiles == own_tile)
     local_term = jnp.where(chosen, local_term, jnp.zeros_like(local_term))
     groups = lax.axis_size("angle")
-    whole = lax.psum(local_term, "angle")
+    whole = local_term
+    for hop in (1, 2, 4):
+        whole = whole + lax.ppermute(whole, "angle", [(dev, dev ^ hop) for dev in range(8)])
     share = whole.shape[2] // groups
     summed = lax.dynamic_slice_in_dim(whole, lax.axis_index("angle") * share, share, 2)
     gradient = summed * (1.0 / groups)

time: 202 us -> 140 us (0.69)
  the two profiles are of different devices: /device:TPU:8 before, /device:TPU:6 now
where the time goes in v1:
time: 140 us; the launch traced here: 139 us
  starting transfers between devices  56.8 us (41%)
  other arithmetic  31.3 us (22%)
  waiting for transfers between devices  28.4 us (20%)
  local copies, waits for them, and re-layouts  17.4 us (12%)
  between operations  5.26 us (4%)
    ppermute x12, starting transfers between devices, from_behind(): return lax.ppermute(value, axis, pairs)  48.8 us
    ppermute x12, waiting for transfers between devices, from_behind(): return lax.ppermute(value, axis, pairs)  21.4 us
    ppermute x3, starting transfers between devices, shards(): lax.ppermute(whole, 'angle', [(dev, dev ^ hop) for dev in range(8)])  7.97 us
    ppermute x3, waiting for transfers between devices, shards(): lax.ppermute(whole, 'angle', [(dev, dev ^ hop) for dev in range(8)])  6.97 us
    sub x15, other arithmetic, rotate_runs(): real_part * cosine - imag_part * sine_full  5.45 us
    slice x6, local copies, waits for them, and re-layouts, next_depth(): field[..., 1:]  4.42 us
    add x3, other arithmetic, shards(): efield = efield + coef * curl_backward(hfield, phases)  3.17 us
  transfers between devices with their start and end apart: 15, of which 10 were waited for; matrix products, arithmetic and copies ran while one was open for 15% of the time, Pallas kernels for 0%

profile of v1, /device:TPU:6, one launch (start us, length us, event | category | flops | bytes accessed | tf_op | source)
XLA Modules:
  0.0 139.2 jit_solution(10067308921561425754)
XLA Ops:
  0.6 1.3 constant_dynamic-update-slice_fusion.1
  2.9 11.1 %collective-permute-start = (f32[2,2,2,8,128]{4,1,0,3,2:T(2,128)}, f32[2,2,2,8,128]{4,1,0,3,2:T(2,128)}, u32[]{:S(2)}, u32[]{:S(2)}) collective-permute-start(f32[2,2,2,8,128]{4,1,0,3,2:T(2,128)} %pad_maximum_fusion.1), channel_id=1, source_target_pairs={{0,3},{1,0},{2,1},{3,2},{4,7},{5,4},{6,5},{7,6},{8,11},{9,8},{10,9... | collective-permute-start | bytes 98312 | tf_op jit(solution)/shard_map/ppermute | solution.py:15
  15.2 6.3 %collective-permute-start.1 = (f32[2,2,2,16,128]{4,1,0,3,2:T(2,128)}, f32[2,2,2,16,128]{4,1,0,3,2:T(2,128)S(1)}, u32[]{:S(2)}, u32[]{:S(2)}) collective-permute-start(f32[2,2,2,16,128]{4,1,0,3,2:T(2,128)} %slice_bitcast_fusion.25), channel_id=1, source_target_pairs={{0,60},{4,0},{8,4},{12,8},{16,12},{20,16},{24,20},{28,24},{32,28},... | collective-permute-start | bytes 196616 | tf_op jit(solution)/shard_map/ppermute | solution.py:15
  24.3 1.1 copy_bitcast_fusion.2
  26.9 0.9 broadcast_divide_fusion
  27.8 1.2 pad_maximum_fusion
  29.6 1.4 compare_reduce_fusion
  32.4 2.0 %slice.554 = f32[2,2,8,16,127]{4,1,0,3,2:T(2,128)} slice(f32[2,2,8,16,128]{4,1,0,3,2:T(2,128)} %copy-done.4), slice={[0:2], [0:2], [0:8], [0:16], [1:128]} | slice | bytes 520192 | tf_op jit(solution)/shard_map/slice | solution.py:29
  34.5 1.7 %slice.547 = f32[2,2,8,15,128]{4,1,0,3,2:T(2,128)} slice(f32[2,2,8,16,128]{4,1,0,3,2:T(2,128)} %get-tuple-element.111), slice={[0:2], [0:2], [0:8], [1:16], [0:128]} | slice | bytes 491520 | tf_op jit(solution)/shard_map/slice | solution.py:51
  36.1 1.6 %slice.557 = f32[2,2,7,16,128]{4,1,0,3,2:T(2,128)} slice(f32[2,2,8,16,128]{4,1,0,3,2:T(2,128)} %get-tuple-element.111), slice={[0:2], [0:2], [1:8], [0:16], [0:128]} | slice | bytes 458752 | tf_op jit(solution)/shard_map/slice | solution.py:54
  37.8 1.0 slice.556
  38.8 1.0 multiply_subtract_fusion.14
  39.8 0.8 maximum_select_fusion.6
  40.9 1.4 %fusion.11 = f32[2,2,1,8,16,128]{5,1,0,4,2,3:T(2,128)S(1)} fusion(f32[2,2,1,1,16,128]{5,1,0,4,3,2:T(2,128)S(1)} %get-tuple-element.82, f32[2,2,1,7,16,128]{5,1,0,4,3,2:T(2,128)} %slice_bitcast_fusion.14, f32[2,2,1,8,1,128]{5,1,0,4,3,2:T(2,128)S(1)} %get-tuple-element.106, f32[2,2,1,8,15,128]{5,1,0,4,3,2:T(2,128)} %slice_bitcast_fusion.8, ...), kind=kLoop, calls=%fused_computation.33 | loop fusion | flops 327680 | bytes 1310720 | tf_op jit(solution)/shard_map/sub | solution.py:57
  43.1 0.9 fusion
  44.2 1.9 %collective-permute-start.3 = (f32[2,2,2,16,128]{4,1,0,3,2:T(2,128)S(1)}, f32[2,2,2,16,128]{4,1,0,3,2:T(2,128)S(1)}, u32[]{:S(2)}, u32[]{:S(2)}) collective-permute-start(f32[2,2,2,16,128]{4,1,0,3,2:T(2,128)S(1)} %slice_bitcast_fusion.24), channel_id=1, source_target_pairs={{0,4},{4,8},{8,12},{12,16},{16,20},{20,24},{24,28},{28,32},{32,36}... | collective-permute-start | bytes 196616 | tf_op jit(solution)/shard_map/ppermute | solution.py:15
  46.1 1.9 %collective-permute-start.2 = (f32[2,2,2,8,128]{4,1,0,3,2:T(2,128)S(1)}, f32[2,2,2,8,128]{4,1,0,3,2:T(2,128)S(1)}, u32[]{:S(2)}, u32[]{:S(2)}) collective-permute-start(f32[2,2,2,8,128]{4,1,0,3,2:T(2,128)S(1)} %pad_maximum_fusion.2), channel_id=1, source_target_pairs={{0,1},{1,2},{2,3},{3,0},{4,5},{5,6},{6,7},{7,4},{8,9},{9,10},{10,1... | collective-permute-start | bytes 98312 | tf_op jit(solution)/shard_map/ppermute | solution.py:15
  48.1 5.9 %collective-permute-done.2 = f32[2,2,2,8,128]{4,1,0,3,2:T(2,128)S(1)} collective-permute-done((f32[2,2,2,8,128]{4,1,0,3,2:T(2,128)S(1)}, f32[2,2,2,8,128]{4,1,0,3,2:T(2,128)S(1)}, u32[]{:S(2)}, u32[]{:S(2)}) %collective-permute-start.2) | collective-permute-done | bytes 32800 | tf_op jit(solution)/shard_map/ppermute | solution.py:15
  54.9 0.8 fusion.14
  55.7 0.8 fusion.1
  56.8 1.1 multiply_subtract_fusion.2
  57.9 1.9 %collective-permute-start.4 = (f32[2,2,2,8,128]{4,1,0,3,2:T(2,128)S(1)}, f32[2,2,2,8,128]{4,1,0,3,2:T(2,128)S(1)}, u32[]{:S(2)}, u32[]{:S(2)}) collective-permute-start(f32[2,2,2,8,128]{4,1,0,3,2:T(2,128)S(1)} %pad_maximum_fusion.3), channel_id=1, source_target_pairs={{0,3},{1,0},{2,1},{3,2},{4,7},{5,4},{6,5},{7,6},{8,11},{9,8},{10,9... | collective-permute-start | bytes 98312 | tf_op jit(solution)/shard_map/ppermute | solution.py:15
  60.6 6.2 %collective-permute-start.5 = (f32[2,2,2,16,128]{4,1,0,3,2:T(2,128)S(1)}, f32[2,2,2,16,128]{4,1,0,3,2:T(2,128)S(1)}, u32[]{:S(2)}, u32[]{:S(2)}) collective-permute-start(f32[2,2,2,16,128]{4,1,0,3,2:T(2,128)S(1)} %slice_bitcast_fusion.23), channel_id=1, source_target_pairs={{0,60},{4,0},{8,4},{12,8},{16,12},{20,16},{24,20},{28,24},{32,28},... | collective-permute-start | bytes 196616 | tf_op jit(solution)/shard_map/ppermute | solution.py:15
  67.0 1.5 %collective-permute-done.5 = f32[2,2,2,16,128]{4,1,0,3,2:T(2,128)S(1)} collective-permute-done((f32[2,2,2,16,128]{4,1,0,3,2:T(2,128)S(1)}, f32[2,2,2,16,128]{4,1,0,3,2:T(2,128)S(1)}, u32[]{:S(2)}, u32[]{:S(2)}) %collective-permute-start.5) | collective-permute-done | bytes 65568 | tf_op jit(solution)/shard_map/ppermute | solution.py:15
  70.4 0.9 copy_subtract_fusion.1
  71.6 4.8 %collective-permute-start.6 = (f32[2,2,2,8,128]{4,3,2,1,0:T(8,128)S(1)}, f32[2,2,2,8,128]{4,3,2,1,0:T(8,128)S(1)}, u32[]{:S(2)}, u32[]{:S(2)}) collective-permute-start(f32[2,2,2,8,128]{4,3,2,1,0:T(8,128)S(1)} %pad_maximum_fusion.4), channel_id=1, source_target_pairs={{0,1},{1,2},{2,3},{3,0},{4,5},{5,6},{6,7},{7,4},{8,9},{9,10},{10,1... | collective-permute-start | bytes 98312 | tf_op jit(solution)/shard_map/ppermute | solution.py:15
  76.4 1.9 %collective-permute-start.7 = (f32[2,2,2,16,128]{4,1,0,3,2:T(2,128)S(1)}, f32[2,2,2,16,128]{4,1,0,3,2:T(2,128)S(1)}, u32[]{:S(2)}, u32[]{:S(2)}) collective-permute-start(f32[2,2,2,16,128]{4,1,0,3,2:T(2,128)S(1)} %bitcast.365), channel_id=1, source_target_pairs={{0,4},{4,8},{8,12},{12,16},{16,20},{20,24},{24,28},{28,32},{32,36}... | collective-permute-start | bytes 196616 | tf_op jit(solution)/shard_map/ppermute | solution.py:15
  78.7 0.8 collective-permute-done.6
  79.7 5.4 %collective-permute-done.7 = f32[2,2,2,16,128]{4,1,0,3,2:T(2,128)S(1)} collective-permute-done((f32[2,2,2,16,128]{4,1,0,3,2:T(2,128)S(1)}, f32[2,2,2,16,128]{4,1,0,3,2:T(2,128)S(1)}, u32[]{:S(2)}, u32[]{:S(2)}) %collective-permute-start.7) | collective-permute-done | bytes 65568 | tf_op jit(solution)/shard_map/ppermute | solution.py:15
  86.4 1.1 fusion.4
  87.7 1.1 multiply_subtract_fusion.1
  88.9 3.1 %collective-permute-start.8 = (f32[2,2,2,8,128]{4,1,0,3,2:T(2,128)S(1)}, f32[2,2,2,8,128]{4,1,0,3,2:T(2,128)S(1)}, u32[]{:S(2)}, u32[]{:S(2)}) collective-permute-start(f32[2,2,2,8,128]{4,1,0,3,2:T(2,128)S(1)} %pad_maximum_fusion.5), channel_id=1, source_target_pairs={{0,3},{1,0},{2,1},{3,2},{4,7},{5,4},{6,5},{7,6},{8,11},{9,8},{10,9... | collective-permute-start | bytes 98312 | tf_op jit(solution)/shard_map/ppermute | solution.py:15
  92.8 3.9 %collective-permute-start.9 = (f32[2,2,2,16,128]{4,1,0,3,2:T(2,128)S(1)}, f32[2,2,2,16,128]{4,1,0,3,2:T(2,128)S(1)}, u32[]{:S(2)}, u32[]{:S(2)}) collective-permute-start(f32[2,2,2,16,128]{4,1,0,3,2:T(2,128)S(1)} %slice_bitcast_fusion.22), channel_id=1, source_target_pairs={{0,60},{4,0},{8,4},{12,8},{16,12},{20,16},{24,20},{28,24},{32,28},... | collective-permute-start | bytes 196616 | tf_op jit(solution)/shard_map/ppermute | solution.py:15
  96.9 2.1 %collective-permute-done.9 = f32[2,2,2,16,128]{4,1,0,3,2:T(2,128)S(1)} collective-permute-done((f32[2,2,2,16,128]{4,1,0,3,2:T(2,128)S(1)}, f32[2,2,2,16,128]{4,1,0,3,2:T(2,128)S(1)}, u32[]{:S(2)}, u32[]{:S(2)}) %collective-permute-start.9) | collective-permute-done | bytes 65568 | tf_op jit(solution)/shard_map/ppermute | solution.py:15
  101.5 3.6 %collective-permute-start.10 = (f32[2,2,2,8,128]{4,3,2,1,0:T(8,128)S(1)}, f32[2,2,2,8,128]{4,3,2,1,0:T(8,128)S(1)}, u32[]{:S(2)}, u32[]{:S(2)}) collective-permute-start(f32[2,2,2,8,128]{4,3,2,1,0:T(8,128)S(1)} %copy.222), channel_id=1, source_target_pairs={{0,1},{1,2},{2,3},{3,0},{4,5},{5,6},{6,7},{7,4},{8,9},{9,10},{10,1... | collective-permute-start | bytes 98312 | tf_op jit(solution)/shard_map/ppermute | solution.py:15
  105.1 2.1 %collective-permute-start.11 = (f32[2,2,2,16,128]{4,1,0,3,2:T(2,128)S(1)}, f32[2,2,2,16,128]{4,1,0,3,2:T(2,128)S(1)}, u32[]{:S(2)}, u32[]{:S(2)}) collective-permute-start(f32[2,2,2,16,128]{4,1,0,3,2:T(2,128)S(1)} %bitcast.364), channel_id=1, source_target_pairs={{0,4},{4,8},{8,12},{12,16},{16,20},{20,24},{24,28},{28,32},{32,36}... | collective-permute-start | bytes 196616 | tf_op jit(solution)/shard_map/ppermute | solution.py:15
  107.6 1.8 %collective-permute-done.10 = f32[2,2,2,8,128]{4,3,2,1,0:T(8,128)S(1)} collective-permute-done((f32[2,2,2,8,128]{4,3,2,1,0:T(8,128)S(1)}, f32[2,2,2,8,128]{4,3,2,1,0:T(8,128)S(1)}, u32[]{:S(2)}, u32[]{:S(2)}) %collective-permute-start.10) | collective-permute-done | bytes 32800 | tf_op jit(solution)/shard_map/ppermute | solution.py:15
  109.5 3.8 %collective-permute-done.11 = f32[2,2,2,16,128]{4,1,0,3,2:T(2,128)S(1)} collective-permute-done((f32[2,2,2,16,128]{4,1,0,3,2:T(2,128)S(1)}, f32[2,2,2,16,128]{4,1,0,3,2:T(2,128)S(1)}, u32[]{:S(2)}, u32[]{:S(2)}) %collective-permute-start.11) | collective-permute-done | bytes 65568 | tf_op jit(solution)/shard_map/ppermute | solution.py:15
  114.7 1.3 fusion.5
  116.0 1.1 multiply_subtract_fusion
  117.1 2.4 %fusion.3 = f32[2,2,3,8,16,128]{5,1,0,4,2,3:T(2,128)S(1)} fusion(f32[2,1,3,8,16,128]{5,1,0,4,2,3:T(1,128)S(1)} %get-tuple-element.40, f32[2,1,3,8,16,128]{5,1,0,4,2,3:T(1,128)S(1)} %get-tuple-element.39, f32[2,1,3,8,16,128]{5,1,0,4,2,3:T(1,128)S(1)} %get-tuple-element.25, f32[2,1,3,8,16,128]{5,1,0,4,2,3:T(1,128)S(1)} %get-tuple-element.24, ...), kind=kLoop, calls=%fused_computation.7 | loop fusion | flops 1179648 | bytes 3932160 | tf_op jit(solution)/shard_map/add | solution.py:116
  120.8 1.9 %collective-permute-start.12 = (f32[8,16,128]{2,1,0:T(8,128)S(1)}, f32[8,16,128]{2,1,0:T(8,128)S(1)}, u32[]{:S(2)}, u32[]{:S(2)}) collective-permute-start(f32[8,16,128]{2,1,0:T(8,128)S(1)} %broadcast_select_fusion), channel_id=1, source_target_pairs={{0,64},{64,0},{128,192},{192,128},{256,320},{320,256},{384,448},{4... | collective-permute-start | bytes 196616 | tf_op jit(solution)/shard_map/ppermute | solution.py:126
  122.7 1.2 collective-permute-done.12
  124.6 2.7 %collective-permute-start.13 = (f32[8,16,128]{2,1,0:T(8,128)S(1)}, f32[8,16,128]{2,1,0:T(8,128)S(1)}, u32[]{:S(2)}, u32[]{:S(2)}) collective-permute-start(f32[8,16,128]{2,1,0:T(8,128)S(1)} %fusion.65), channel_id=1, source_target_pairs={{0,128},{64,192},{128,0},{192,64},{256,384},{320,448},{384,256},{4... | collective-permute-start | bytes 196616 | tf_op jit(solution)/shard_map/ppermute | solution.py:126
  127.4 3.4 %collective-permute-done.13 = f32[8,16,128]{2,1,0:T(8,128)S(1)} collective-permute-done((f32[8,16,128]{2,1,0:T(8,128)S(1)}, f32[8,16,128]{2,1,0:T(8,128)S(1)}, u32[]{:S(2)}, u32[]{:S(2)}) %collective-permute-start.13) | collective-permute-done | bytes 65568 | tf_op jit(solution)/shard_map/ppermute | solution.py:126
  130.8 3.3 %collective-permute-start.14 = (f32[8,16,128]{2,1,0:T(8,128)S(1)}, f32[8,16,128]{2,1,0:T(8,128)S(1)}, u32[]{:S(2)}, u32[]{:S(2)}) collective-permute-start(f32[8,16,128]{2,1,0:T(8,128)S(1)} %add.140), channel_id=1, source_target_pairs={{0,256},{64,320},{128,384},{192,448},{256,0},{320,64},{384,128},{4... | collective-permute-start | bytes 196616 | tf_op jit(solution)/shard_map/ppermute | solution.py:126
  134.6 0.8 copy.232
  136.1 2.3 %collective-permute-done.14 = f32[8,16,128]{2,1,0:T(8,128)S(1)} collective-permute-done((f32[8,16,128]{2,1,0:T(8,128)S(1)}, f32[8,16,128]{2,1,0:T(8,128)S(1)}, u32[]{:S(2)}, u32[]{:S(2)}) %collective-permute-start.14) | collective-permute-done | bytes 65568 | tf_op jit(solution)/shard_map/ppermute | solution.py:126
  (149 shorter events, 21.2 us)
Async XLA Ops:
  0.6 1.4 copy-start.9
  2.9 19.4 %copy-start.10 = (f32[8,2]{0,1:T(2,128)S(1)}, f32[8,2]{0,1:T(2,128)}, u32[]{:S(2)}) copy-start(f32[8,2]{0,1:T(2,128)} %param.14) | copy-start | bytes 196
  2.9 36.0 %collective-permute-start = (f32[2,2,2,8,128]{4,1,0,3,2:T(2,128)}, f32[2,2,2,8,128]{4,1,0,3,2:T(2,128)}, u32[]{:S(2)}, u32[]{:S(2)}) collective-permute-start(f32[2,2,2,8,128]{4,1,0,3,2:T(2,128)} %pad_maximum_fusion.1), channel_id=1, source_target_pairs={{0,3},{1,0},{2,1},{3,2},{4,7},{5,4},{6,5},{7,6},{8,11},{9,8},{10,9... | collective-permute-start | bytes 98312 | tf_op jit(solution)/shard_map/ppermute | solution.py:15
  15.2 25.4 %collective-permute-start.1 = (f32[2,2,2,16,128]{4,1,0,3,2:T(2,128)}, f32[2,2,2,16,128]{4,1,0,3,2:T(2,128)S(1)}, u32[]{:S(2)}, u32[]{:S(2)}) collective-permute-start(f32[2,2,2,16,128]{4,1,0,3,2:T(2,128)} %slice_bitcast_fusion.25), channel_id=1, source_target_pairs={{0,60},{4,0},{8,4},{12,8},{16,12},{20,16},{24,20},{28,24},{32,28},... | collective-permute-start | bytes 196616 | tf_op jit(solution)/shard_map/ppermute | solution.py:15
  21.5 5.4 %copy-start = (f32[2,2,1,8,16,128]{5,4,3,2,1,0:T(8,128)}, f32[2,2,1,8,16,128]{5,4,3,2,1,0:T(8,128)S(1)}, u32[]{:S(2)}) copy-start(f32[2,2,1,8,16,128]{5,4,3,2,1,0:T(8,128)S(1)} %get-tuple-element.49) | copy-start | bytes 786436
  21.6 5.4 %copy-start.2 = (f32[2,2,8,16,128]{4,1,0,3,2:T(2,128)}, f32[2,2,8,16,128]{4,1,0,3,2:T(2,128)S(1)}, u32[]{:S(2)}) copy-start(f32[2,2,8,16,128]{4,1,0,3,2:T(2,128)S(1)} %slice_bitcast_fusion.21) | copy-start | bytes 786436
  25.4 1.5 %copy-start.4 = (f32[2,2,8,16,128]{4,1,0,3,2:T(2,128)}, f32[2,2,8,16,128]{4,1,0,3,2:T(2,128)S(1)}, u32[]{:S(2)}) copy-start(f32[2,2,8,16,128]{4,1,0,3,2:T(2,128)S(1)} %get-tuple-element.112) | copy-start | bytes 786436
  32.4 5.3 %copy-start.3 = (f32[2,2,8,16,128]{4,1,0,3,2:T(2,128)S(1)}, f32[2,2,8,16,128]{4,1,0,3,2:T(2,128)}, u32[]{:S(2)}) copy-start(f32[2,2,8,16,128]{4,1,0,3,2:T(2,128)} %copy-done.2) | copy-start | bytes 786436
  38.8 3.5 %copy-start.1 = (f32[2,2,1,8,16,128]{5,4,3,2,1,0:T(8,128)S(1)}, f32[2,2,1,8,16,128]{5,4,3,2,1,0:T(8,128)}, u32[]{:S(2)}) copy-start(f32[2,2,1,8,16,128]{5,4,3,2,1,0:T(8,128)} %copy-done) | copy-start | bytes 786436
  38.8 3.5 %copy-start.5 = (f32[2,2,8,16,127]{4,1,0,3,2:T(2,128)S(1)}, f32[2,2,8,16,127]{4,1,0,3,2:T(2,128)}, u32[]{:S(2)}) copy-start(f32[2,2,8,16,127]{4,1,0,3,2:T(2,128)} %slice.554) | copy-start | bytes 780292
  38.8 3.5 %copy-start.6 = (f32[2,2,8,16,127]{4,1,0,3,2:T(2,128)S(1)}, f32[2,2,8,16,127]{4,1,0,3,2:T(2,128)}, u32[]{:S(2)}) copy-start(f32[2,2,8,16,127]{4,1,0,3,2:T(2,128)} %slice.556) | copy-start | bytes 780292
  38.8 3.5 %copy-start.7 = (f32[2,2,8,15,128]{4,1,0,3,2:T(2,128)S(1)}, f32[2,2,8,15,128]{4,1,0,3,2:T(2,128)}, u32[]{:S(2)}) copy-start(f32[2,2,8,15,128]{4,1,0,3,2:T(2,128)} %slice.547) | copy-start | bytes 737284
  38.8 3.5 %copy-start.8 = (f32[2,2,7,16,128]{4,1,0,3,2:T(2,128)S(1)}, f32[2,2,7,16,128]{4,1,0,3,2:T(2,128)}, u32[]{:S(2)}) copy-start(f32[2,2,7,16,128]{4,1,0,3,2:T(2,128)} %slice.557) | copy-start | bytes 688132
  44.2 10.0 %collective-permute-start.3 = (f32[2,2,2,16,128]{4,1,0,3,2:T(2,128)S(1)}, f32[2,2,2,16,128]{4,1,0,3,2:T(2,128)S(1)}, u32[]{:S(2)}, u32[]{:S(2)}) collective-permute-start(f32[2,2,2,16,128]{4,1,0,3,2:T(2,128)S(1)} %slice_bitcast_fusion.24), channel_id=1, source_target_pairs={{0,4},{4,8},{8,12},{12,16},{16,20},{20,24},{24,28},{28,32},{32,36}... | collective-permute-start | bytes 196616 | tf_op jit(solution)/shard_map/ppermute | solution.py:15
  46.1 7.9 %collective-permute-start.2 = (f32[2,2,2,8,128]{4,1,0,3,2:T(2,128)S(1)}, f32[2,2,2,8,128]{4,1,0,3,2:T(2,128)S(1)}, u32[]{:S(2)}, u32[]{:S(2)}) collective-permute-start(f32[2,2,2,8,128]{4,1,0,3,2:T(2,128)S(1)} %pad_maximum_fusion.2), channel_id=1, source_target_pairs={{0,1},{1,2},{2,3},{3,0},{4,5},{5,6},{6,7},{7,4},{8,9},{9,10},{10,1... | collective-permute-start | bytes 98312 | tf_op jit(solution)/shard_map/ppermute | solution.py:15
  57.9 8.9 %collective-permute-start.4 = (f32[2,2,2,8,128]{4,1,0,3,2:T(2,128)S(1)}, f32[2,2,2,8,128]{4,1,0,3,2:T(2,128)S(1)}, u32[]{:S(2)}, u32[]{:S(2)}) collective-permute-start(f32[2,2,2,8,128]{4,1,0,3,2:T(2,128)S(1)} %pad_maximum_fusion.3), channel_id=1, source_target_pairs={{0,3},{1,0},{2,1},{3,2},{4,7},{5,4},{6,5},{7,6},{8,11},{9,8},{10,9... | collective-permute-start | bytes 98312 | tf_op jit(solution)/shard_map/ppermute | solution.py:15
  60.6 7.9 %collective-permute-start.5 = (f32[2,2,2,16,128]{4,1,0,3,2:T(2,128)S(1)}, f32[2,2,2,16,128]{4,1,0,3,2:T(2,128)S(1)}, u32[]{:S(2)}, u32[]{:S(2)}) collective-permute-start(f32[2,2,2,16,128]{4,1,0,3,2:T(2,128)S(1)} %slice_bitcast_fusion.23), channel_id=1, source_target_pairs={{0,60},{4,0},{8,4},{12,8},{16,12},{20,16},{24,20},{28,24},{32,28},... | collective-permute-start | bytes 196616 | tf_op jit(solution)/shard_map/ppermute | solution.py:15
  71.6 7.9 %collective-permute-start.6 = (f32[2,2,2,8,128]{4,3,2,1,0:T(8,128)S(1)}, f32[2,2,2,8,128]{4,3,2,1,0:T(8,128)S(1)}, u32[]{:S(2)}, u32[]{:S(2)}) collective-permute-start(f32[2,2,2,8,128]{4,3,2,1,0:T(8,128)S(1)} %pad_maximum_fusion.4), channel_id=1, source_target_pairs={{0,1},{1,2},{2,3},{3,0},{4,5},{5,6},{6,7},{7,4},{8,9},{9,10},{10,1... | collective-permute-start | bytes 98312 | tf_op jit(solution)/shard_map/ppermute | solution.py:15
  76.4 8.6 %collective-permute-start.7 = (f32[2,2,2,16,128]{4,1,0,3,2:T(2,128)S(1)}, f32[2,2,2,16,128]{4,1,0,3,2:T(2,128)S(1)}, u32[]{:S(2)}, u32[]{:S(2)}) collective-permute-start(f32[2,2,2,16,128]{4,1,0,3,2:T(2,128)S(1)} %bitcast.365), channel_id=1, source_target_pairs={{0,4},{4,8},{8,12},{12,16},{16,20},{20,24},{24,28},{28,32},{32,36}... | collective-permute-start | bytes 196616 | tf_op jit(solution)/shard_map/ppermute | solution.py:15
  88.9 7.8 %collective-permute-start.8 = (f32[2,2,2,8,128]{4,1,0,3,2:T(2,128)S(1)}, f32[2,2,2,8,128]{4,1,0,3,2:T(2,128)S(1)}, u32[]{:S(2)}, u32[]{:S(2)}) collective-permute-start(f32[2,2,2,8,128]{4,1,0,3,2:T(2,128)S(1)} %pad_maximum_fusion.5), channel_id=1, source_target_pairs={{0,3},{1,0},{2,1},{3,2},{4,7},{5,4},{6,5},{7,6},{8,11},{9,8},{10,9... | collective-permute-start | bytes 98312 | tf_op jit(solution)/shard_map/ppermute | solution.py:15
  92.8 6.2 %collective-permute-start.9 = (f32[2,2,2,16,128]{4,1,0,3,2:T(2,128)S(1)}, f32[2,2,2,16,128]{4,1,0,3,2:T(2,128)S(1)}, u32[]{:S(2)}, u32[]{:S(2)}) collective-permute-start(f32[2,2,2,16,128]{4,1,0,3,2:T(2,128)S(1)} %slice_bitcast_fusion.22), channel_id=1, source_target_pairs={{0,60},{4,0},{8,4},{12,8},{16,12},{20,16},{24,20},{28,24},{32,28},... | collective-permute-start | bytes 196616 | tf_op jit(solution)/shard_map/ppermute | solution.py:15
  101.5 7.9 %collective-permute-start.10 = (f32[2,2,2,8,128]{4,3,2,1,0:T(8,128)S(1)}, f32[2,2,2,8,128]{4,3,2,1,0:T(8,128)S(1)}, u32[]{:S(2)}, u32[]{:S(2)}) collective-permute-start(f32[2,2,2,8,128]{4,3,2,1,0:T(8,128)S(1)} %copy.222), channel_id=1, source_target_pairs={{0,1},{1,2},{2,3},{3,0},{4,5},{5,6},{6,7},{7,4},{8,9},{9,10},{10,1... | collective-permute-start | bytes 98312 | tf_op jit(solution)/shard_map/ppermute | solution.py:15
  105.1 8.3 %collective-permute-start.11 = (f32[2,2,2,16,128]{4,1,0,3,2:T(2,128)S(1)}, f32[2,2,2,16,128]{4,1,0,3,2:T(2,128)S(1)}, u32[]{:S(2)}, u32[]{:S(2)}) collective-permute-start(f32[2,2,2,16,128]{4,1,0,3,2:T(2,128)S(1)} %bitcast.364), channel_id=1, source_target_pairs={{0,4},{4,8},{8,12},{12,16},{16,20},{20,24},{24,28},{28,32},{32,36}... | collective-permute-start | bytes 196616 | tf_op jit(solution)/shard_map/ppermute | solution.py:15
  120.8 3.1 %collective-permute-start.12 = (f32[8,16,128]{2,1,0:T(8,128)S(1)}, f32[8,16,128]{2,1,0:T(8,128)S(1)}, u32[]{:S(2)}, u32[]{:S(2)}) collective-permute-start(f32[8,16,128]{2,1,0:T(8,128)S(1)} %broadcast_select_fusion), channel_id=1, source_target_pairs={{0,64},{64,0},{128,192},{192,128},{256,320},{320,256},{384,448},{4... | collective-permute-start | bytes 196616 | tf_op jit(solution)/shard_map/ppermute | solution.py:126
  124.6 6.2 %collective-permute-start.13 = (f32[8,16,128]{2,1,0:T(8,128)S(1)}, f32[8,16,128]{2,1,0:T(8,128)S(1)}, u32[]{:S(2)}, u32[]{:S(2)}) collective-permute-start(f32[8,16,128]{2,1,0:T(8,128)S(1)} %fusion.65), channel_id=1, source_target_pairs={{0,128},{64,192},{128,0},{192,64},{256,384},{320,448},{384,256},{4... | collective-permute-start | bytes 196616 | tf_op jit(solution)/shard_map/ppermute | solution.py:126
  130.8 7.7 %collective-permute-start.14 = (f32[8,16,128]{2,1,0:T(8,128)S(1)}, f32[8,16,128]{2,1,0:T(8,128)S(1)}, u32[]{:S(2)}, u32[]{:S(2)}) collective-permute-start(f32[8,16,128]{2,1,0:T(8,128)S(1)} %add.140), channel_id=1, source_target_pairs={{0,256},{64,320},{128,384},{192,448},{256,0},{320,64},{384,128},{4... | collective-permute-start | bytes 196616 | tf_op jit(solution)/shard_map/ppermute | solution.py:126
